TPU v7x, 32 devices: a whole 2x2x4 slice. The times are simulated.
32 devices in a mesh: cells: 8 (over y, x, core), obs: 4 (over z).
Axes of the slice: x: 2, y: 2, z: 4, core: 2. Of those that a mesh axis runs over, the one named last changes fastest.
Arguments:
- histories: bfloat16 [64, 384], P('obs'), may hold values from -6 to 6
- amplitude: bfloat16 [64, 5, 8192], P('obs', None, 'cells'), may hold values from -0.75 to 0.75
- weights: bfloat16 [8192, 256], P('cells'), may hold values from -0.375 to 0.375
- retarded: int32 [64, 64], P('obs', 'cells'), may hold values from 0 to 128
- owner_block: int32 [8192], P('cells'), may hold values from 0 to 7, as said below
- owner_cell: int32 [8192], P('cells'), may hold values from 0 to 16383
- adjoint: float32 [5, 16, 64, 128], P(None, 'cells', 'obs'), may hold values from -6 to 6
- step_size: float32 [16, 64, 128], P('cells', 'obs'), may hold values from 0.1 to 0.6
- jacobian: float32 [8, 3, 5, 5], P('cells'), may hold values from -6 to 6
Outputs:
- adjoint_next: float32 [5, 16, 64, 128], P(None, 'cells', 'obs')
- panel_source: float32 [5, 8192], P(None, 'cells')
Inputs may be any that keep to these rules, and one draw needn't show every extreme that they name: `owner_block`: among each device's 1024 panels at most 512 name one owner block; one owner block, drawn from the seed, is named by exactly 512 panels of every device.
All inputs are finite; a program needn't handle non-finite values.
Results may differ from a plain program's by a relative error of at most 0.0003.
Values sent between devices are 32-bit elements; how exact they have to be, the bound alone decides.
A program may use at most 192 MiB of HBM per device.

v0:
```python
import jax
import jax.numpy as jnp
from jax import lax
from jax.sharding import PartitionSpec as P

SAMPLES = 256
SPAN = 128
COMP = 5
TILE = 128
smoothing = 0.25


def extended(cells, sides, width, closed):
    for axis, dim in sides:
        count = lax.axis_size(axis)
        ends = count if closed else count - 1
        head = lax.slice_in_dim(cells, 0, width, axis=dim)
        tail = lax.slice_in_dim(cells, cells.shape[dim] - width, cells.shape[dim], axis=dim)
        cells = jnp.concatenate(
            [
                lax.ppermute(tail, axis, [(i, (i + 1) % count) for i in range(ends)]),
                cells,
                lax.ppermute(head, axis, [((i + 1) % count, i) for i in range(ends)]),
            ],
            axis=dim,
        )
    return cells


def on_device(
    histories, amplitude, weights, retarded, owner_block, owner_cell, adjoint, step_size, jacobian
):
    tile_count = weights.shape[0] // TILE
    weights_tiled = weights.reshape(tile_count, TILE, SAMPLES)
    observers_local = histories.shape[0]
    history_len = histories.shape[1]
    shifted = jnp.broadcast_to(histories[:, None, :], (observers_local, tile_count, history_len))
    for bit_number in range(SPAN.bit_length()):
        amount = 1 << bit_number
        moved = jnp.concatenate(
            [
                shifted[..., amount:],
                jnp.zeros((observers_local, tile_count, amount), shifted.dtype),
            ],
            axis=2,
        )
        chosen = retarded >> bit_number & 1 == 1
        shifted = jnp.where(chosen[:, :, None], moved, shifted)
    window = shifted[..., :SAMPLES]
    projected = jnp.einsum(
        "tps,ots->otp", weights_tiled, window, preferred_element_type=jnp.float32
    )
    projected = projected.reshape(projected.shape[0], -1)
    partial_value = jnp.sum(amplitude.astype(jnp.float32) * projected[:, None, :], axis=0)
    panel_source = lax.psum(partial_value, "obs")
    my_block = lax.axis_index("cells")
    my_group = lax.axis_index("obs")
    azimuth_local = adjoint.shape[1]
    radial_local = adjoint.shape[2]
    axial_len = adjoint.shape[3]
    radial_all = radial_local * lax.axis_size("obs")
    block_cells = azimuth_local * radial_all * axial_len
    device_cells = azimuth_local * radial_local * axial_len
    target = (owner_block * block_cells + owner_cell).reshape(1, -1)
    empty_field = jnp.zeros((COMP, device_cells), jnp.float32)
    devices = lax.axis_size("cells")
    capacity = 4 * owner_block.shape[0] // devices
    one_hot = (owner_block[:, None] == jnp.arange(devices, dtype=jnp.int32)[None, :]).astype(
        jnp.int32
    )
    slot_rank = jnp.sum(jnp.cumsum(one_hot, axis=0) * one_hot, axis=1) - 1
    slot_of = owner_block * capacity + slot_rank
    outgoing = jnp.zeros((COMP, devices * capacity), jnp.float32).at[:, slot_of].set(panel_source)
    out_index = jnp.full((1, devices * capacity), -1, jnp.int32).at[0, slot_of].set(target[0])
    received, arrivals = (
        lax.all_to_all(outgoing, "cells", split_axis=1, concat_axis=1, tiled=True),
        lax.all_to_all(out_index, "cells", split_axis=1, concat_axis=1, tiled=True),
    )
    flat_index = arrivals[0]
    block_of = flat_index // block_cells
    within = flat_index % block_cells
    azimuth = within // (radial_all * axial_len)
    radius = within // axial_len % radial_all
    axial = within % axial_len
    is_mine = (block_of == my_block) & (radius // radial_local == my_group) & (flat_index >= 0)
    position = (azimuth * radial_local + radius - my_group * radial_local) * axial_len + axial
    landing = jnp.where(is_mine, position, device_cells)
    surface = empty_field.at[:, landing].add(received, mode="drop")
    widened = extended(adjoint, (("cells", 1),), 1, True)
    heightened = extended(adjoint, (("obs", 2),), 1, False)
    deepened = jnp.pad(adjoint, ((0, 0), (0, 0), (0, 0), (1, 1)))
    matrices = jacobian[0]
    neighbours = (
        (widened[:, 2:], widened[:, :-2]),
        (heightened[:, :, 2:], heightened[:, :, :-2]),
        (deepened[..., 2:], deepened[..., :-2]),
    )
    summed = jnp.zeros_like(adjoint)
    for direction in range(3):
        forward, backward = neighbours[direction]
        rotated = jnp.einsum(
            "kc,karz->carz",
            matrices[direction],
            forward - backward,
            precision=lax.Precision.HIGHEST,
        )
        summed = summed + (0.5 * rotated + smoothing * (forward - 2.0 * adjoint + backward))
    adjoint_next = adjoint + step_size[None] * summed + surface.reshape(adjoint.shape)
    return (adjoint_next, panel_source)


def solution(mesh):
    return jax.shard_map(
        on_device,
        mesh=mesh,
        in_specs=(
            P("obs", None),
            P("obs", None, "cells"),
            P("cells", None),
            P("obs", "cells"),
            P("cells"),
            P("cells"),
            P(None, "cells", "obs", None),
            P("cells", "obs", None),
            P("cells", None, None, None),
        ),
        out_specs=(P(None, "cells", "obs", None), P(None, "cells")),
        check_vma=False,
    )
```

profile of v0, /device:TPU:0, one launch (start us, length us, event | category | flops | bytes accessed | tf_op | source)
XLA Modules:
  0.0 93.0 jit_solution(10608358137834040790)
XLA Ops:
  0.6 0.8 fusion.22
  1.4 2.3 %reduce-window.6 = s32[8,8,128]{2,1,0:T(8,128)S(1)} reduce-window(s32[8,8,128]{2,1,0:T(8,128)S(1)} %fusion.22, s32[]{:T(128)} %constant.118.clone.1), window={size=1x1x128 pad=0_0x0_0x127_0}, to_apply=%region_0.1 | reduce-window | flops 1040384 | bytes 65540 | tf_op jit(solution)/shard_map/reduce-window
  4.2 0.7 fusion.21
  5.6 0.7 fusion.25
  6.3 0.7 and_reduce_fusion
  7.1 4.9 %scatter_custom_fusion.2 = s32[4096]{0:T(1024)} fusion(s32[1024]{0:T(1024)S(1)} %broadcast_select_fusion, s32[1024]{0:T(1024)S(1)} %get-tuple-element.25, s32[]{:T(128)} %constant.116.clone.1), kind=kCustom, calls=%fused_computation.79 | custom fusion | bytes 16388
  12.0 5.2 %all-to-all-start = ((s32[1,8,512]{2,0,1:T(1,128)}), s32[1,8,512]{2,0,1:T(1,128)S(1)}, u32[]{:S(2)}, u32[]{:S(2)}) async-start(s32[1,8,512]{2,0,1:T(1,128)} %bitcast.12), calls=%async_computation | async-start | bytes 32768 | tf_op jit(solution)/shard_map/all_to_all | solution.py:77
  17.2 0.9 %copy.91 = f32[5,2,16,128]{3,0,2,1:T(8,128)S(1)} copy(f32[5,2,16,128]{3,2,1,0:T(8,128)} %param.15) | data formatting | bytes 163840 | tf_op args[6]
  18.1 1.3 %collective-permute-start.2 = (f32[5,2,1,128]{3,0,2,1:T(8,128)S(1)}, f32[5,2,1,128]{3,0,2,1:T(8,128)}, u32[]{:S(2)}, u32[]{:S(2)}) collective-permute-start(f32[5,2,1,128]{3,0,2,1:T(8,128)S(1)} %get-tuple-element.13), channel_id=1, source_target_pairs={{1,0},{2,1},{3,2},{5,4},{6,5},{7,6},{9,8},{10,9},{11,10},{13,12},{... | collective-permute-start | bytes 15368 | tf_op jit(solution)/shard_map/ppermute | solution.py:23
  19.4 5.1 %collective-permute-start.3 = (f32[5,2,1,128]{3,0,2,1:T(8,128)S(1)}, f32[5,2,1,128]{3,0,2,1:T(8,128)}, u32[]{:S(2)}, u32[]{:S(2)}) collective-permute-start(f32[5,2,1,128]{3,0,2,1:T(8,128)S(1)} %get-tuple-element.12), channel_id=1, source_target_pairs={{0,1},{1,2},{2,3},{4,5},{5,6},{6,7},{8,9},{9,10},{10,11},{12,13},{... | collective-permute-start | bytes 15368 | tf_op jit(solution)/shard_map/ppermute | solution.py:21
  25.2 2.1 %collective-permute-start = (f32[5,1,16,128]{3,0,2,1:T(8,128)}, f32[5,1,16,128]{3,0,2,1:T(8,128)S(1)}, u32[]{:S(2)}, u32[]{:S(2)}) collective-permute-start(f32[5,1,16,128]{3,0,2,1:T(8,128)} %get-tuple-element.11), channel_id=1, source_target_pairs={{4,0},{8,4},{12,8},{16,12},{20,16},{24,20},{28,24},{0,28},{5,1},{9... | collective-permute-start | bytes 122888 | tf_op jit(solution)/shard_map/ppermute | solution.py:23
  28.0 0.8 slice.95
  28.8 0.8 pad_select_fusion.6
  29.7 0.9 pad_select_fusion.5
  30.7 0.8 pad_select_fusion.4
  32.7 1.1 %fusion.10 = f32[5,2,16,128]{3,0,2,1:T(8,128)} fusion(f32[5,2,16,128]{3,0,2,1:T(8,128)S(1)} %copy.91, f32[1,1,5,5]{3,0,2,1:T(1,128)S(1)} %get-tuple-element.16), kind=kOutput, calls=%fused_computation.16 | convolution fusion | flops 1372160 | bytes 346624 | tf_op jit(solution)/shard_map/kc,karz->carz/dot_general | solution.py:101
  33.8 17.3 %psum.7 = f32[5,1024]{1,0:T(8,128)S(1)} all-reduce(f32[5,1024]{1,0:T(8,128)S(1)} %multiply_reduce_fusion), channel_id=1, replica_groups=mesh['cells'=8,'obs'=4] {'obs'}, use_global_device_ids=true, to_apply=%region_5.6 | all-reduce | flops 5120 | bytes 40960 | tf_op jit(solution)/shard_map/psum | solution.py:55
  51.4 3.6 %scatter_custom_fusion = f32[5,4096]{0,1:T(8,128)S(1)} fusion(s32[1024]{0:T(1024)S(1)} %get-tuple-element.26, f32[1024,5]{1,0:T(8,128)S(1)} %copy.93, f32[]{:T(128)} %constant.115.clone.1), kind=kCustom, calls=%fused_computation.20 | custom fusion | bytes 81924 | tf_op jit(solution)/shard_map/scatter | solution.py:73
  55.0 1.3 %copy.94 = f32[5,8,512]{2,0,1:T(8,128)} copy(f32[5,8,512]{0,2,1:T(8,128)S(1)} %bitcast.73) | data formatting | bytes 163840 | tf_op jit(solution)/shard_map/all_to_all | solution.py:76
  56.3 1.1 %fusion.9 = f32[5,2,16,128]{3,0,2,1:T(8,128)S(1)} fusion(f32[5,2,1,128]{3,0,2,1:T(8,128)} %collective-permute-done.2, f32[5,2,16,128]{3,0,2,1:T(8,128)S(1)} %copy.91, f32[5,2,1,128]{3,0,2,1:T(8,128)} %collective-permute-done.3, f32[1,1,5,5]{3,0,2,1:T(1,128)S(1)} %get-tuple-element.15), kind=kOutput, calls=%fused_computation.15 | convolution fusion | flops 1454080 | bytes 174180 | tf_op jit(solution)/shard_map/kc,karz->carz/dot_general | solution.py:101
  57.4 3.4 %all-to-all-start.1 = ((f32[5,8,512]{2,0,1:T(8,128)}), f32[5,8,512]{2,0,1:T(8,128)S(1)}, u32[]{:S(2)}, u32[]{:S(2)}) async-start(f32[5,8,512]{2,0,1:T(8,128)} %copy.94), calls=%async_computation.1 | async-start | bytes 262144 | tf_op jit(solution)/shard_map/all_to_all | solution.py:76
  61.3 5.0 %all-to-all-done.1 = f32[5,8,512]{2,0,1:T(8,128)S(1)} async-done(((f32[5,8,512]{2,0,1:T(8,128)}), f32[5,8,512]{2,0,1:T(8,128)S(1)}, u32[]{:S(2)}, u32[]{:S(2)}) %all-to-all-start.1) | async-done | bytes 81952 | tf_op jit(solution)/shard_map/all_to_all | solution.py:76
  66.2 2.0 %copy.95 = f32[4096,5]{1,0:T(8,128)} copy(f32[4096,5]{0,1:T(8,128)S(1)} %bitcast.74) | data formatting | bytes 163840 | tf_op jit(solution)/shard_map/all_to_all | solution.py:76
  68.2 23.2 %scatter_custom_fusion.1 = f32[5,4096]{0,1:T(8,128)S(1)} fusion(s32[4096]{0:T(1024)S(1)} %bitcast.82, f32[4096,5]{1,0:T(8,128)} %copy.95, f32[]{:T(128)} %constant.115.clone.1), kind=kCustom, calls=%fused_computation.18 | custom fusion | flops 20480 | bytes 82432 | tf_op jit(solution)/shard_map/scatter-add | solution.py:88
  (47 shorter events, 6.3 us)
Async XLA Ops:
  0.6 31.7 %copy-start = (bf16[1024,256]{1,0:T(8,128)(2,1)S(1)}, bf16[1024,256]{1,0:T(8,128)(2,1)}, u32[]{:S(2)}) copy-start(bf16[1024,256]{1,0:T(8,128)(2,1)} %param.11) | copy-start | bytes 1572868
  12.0 45.4 %all-to-all-start = ((s32[1,8,512]{2,0,1:T(1,128)}), s32[1,8,512]{2,0,1:T(1,128)S(1)}, u32[]{:S(2)}, u32[]{:S(2)}) async-start(s32[1,8,512]{2,0,1:T(1,128)} %bitcast.12), calls=%async_computation | async-start | bytes 32768 | tf_op jit(solution)/shard_map/all_to_all | solution.py:77
  18.1 38.1 %collective-permute-start.2 = (f32[5,2,1,128]{3,0,2,1:T(8,128)S(1)}, f32[5,2,1,128]{3,0,2,1:T(8,128)}, u32[]{:S(2)}, u32[]{:S(2)}) collective-permute-start(f32[5,2,1,128]{3,0,2,1:T(8,128)S(1)} %get-tuple-element.13), channel_id=1, source_target_pairs={{1,0},{2,1},{3,2},{5,4},{6,5},{7,6},{9,8},{10,9},{11,10},{13,12},{... | collective-permute-start | bytes 15368 | tf_op jit(solution)/shard_map/ppermute | solution.py:23
  19.4 36.9 %collective-permute-start.3 = (f32[5,2,1,128]{3,0,2,1:T(8,128)S(1)}, f32[5,2,1,128]{3,0,2,1:T(8,128)}, u32[]{:S(2)}, u32[]{:S(2)}) collective-permute-start(f32[5,2,1,128]{3,0,2,1:T(8,128)S(1)} %get-tuple-element.12), channel_id=1, source_target_pairs={{0,1},{1,2},{2,3},{4,5},{5,6},{6,7},{8,9},{9,10},{10,11},{12,13},{... | collective-permute-start | bytes 15368 | tf_op jit(solution)/shard_map/ppermute | solution.py:21
  25.2 66.8 %collective-permute-start = (f32[5,1,16,128]{3,0,2,1:T(8,128)}, f32[5,1,16,128]{3,0,2,1:T(8,128)S(1)}, u32[]{:S(2)}, u32[]{:S(2)}) collective-permute-start(f32[5,1,16,128]{3,0,2,1:T(8,128)} %get-tuple-element.11), channel_id=1, source_target_pairs={{4,0},{8,4},{12,8},{16,12},{20,16},{24,20},{28,24},{0,28},{5,1},{9... | collective-permute-start | bytes 122888 | tf_op jit(solution)/shard_map/ppermute | solution.py:23
  27.3 64.7 %collective-permute-start.1 = (f32[5,1,16,128]{3,0,2,1:T(8,128)S(1)}, f32[5,1,16,128]{3,0,2,1:T(8,128)S(1)}, u32[]{:S(2)}, u32[]{:S(2)}) collective-permute-start(f32[5,1,16,128]{3,0,2,1:T(8,128)S(1)} %get-tuple-element.10), channel_id=1, source_target_pairs={{0,4},{4,8},{8,12},{12,16},{16,20},{20,24},{24,28},{28,0},{1,5},{5... | collective-permute-start | bytes 122888 | tf_op jit(solution)/shard_map/ppermute | solution.py:21
  28.8 3.9 %copy-start.5 = (f32[1,3,5,5]{3,0,2,1:T(1,128)S(1)}, f32[1,3,5,5]{3,0,2,1:T(1,128)}, u32[]{:S(2)}) copy-start(f32[1,3,5,5]{3,0,2,1:T(1,128)} %param.17) | copy-start | bytes 904
  29.7 4.0 %copy-start.1 = (bf16[16,5,1024]{2,0,1:T(8,128)(2,1)S(1)}, bf16[16,5,1024]{2,0,1:T(8,128)(2,1)}, u32[]{:S(2)}) copy-start(bf16[16,5,1024]{2,0,1:T(8,128)(2,1)} %param.10) | copy-start | bytes 491524
  51.2 5.1 %copy-start.2 = (f32[5,1024]{1,0:T(8,128)}, f32[5,1024]{1,0:T(8,128)S(1)}, u32[]{:S(2)}) copy-start(f32[5,1024]{1,0:T(8,128)S(1)} %psum.7) | copy-start | bytes 61444
  57.4 8.8 %all-to-all-start.1 = ((f32[5,8,512]{2,0,1:T(8,128)}), f32[5,8,512]{2,0,1:T(8,128)S(1)}, u32[]{:S(2)}, u32[]{:S(2)}) async-start(f32[5,8,512]{2,0,1:T(8,128)} %copy.94), calls=%async_computation.1 | async-start | bytes 262144 | tf_op jit(solution)/shard_map/all_to_all | solution.py:76
  68.2 23.8 %copy-start.3 = (f32[5,2,16,128]{3,0,2,1:T(8,128)S(1)}, f32[5,2,16,128]{3,0,2,1:T(8,128)}, u32[]{:S(2)}) copy-start(f32[5,2,16,128]{3,0,2,1:T(8,128)} %fusion.10) | copy-start | bytes 245764
  68.2 23.8 %copy-start.4 = (f32[2,16,128]{2,1,0:T(8,128)S(1)}, f32[2,16,128]{2,1,0:T(8,128)}, u32[]{:S(2)}) copy-start(f32[2,16,128]{2,1,0:T(8,128)} %param.16) | copy-start | bytes 49156
where the time goes:
time: 94.1 us; the launch traced here: 93 us
  other arithmetic  33.4 us (35%)
  blocking collectives  17.3 us (18%)
  starting transfers between devices  17.1 us (18%)
  local copies, waits for them, and re-layouts  16.5 us (18%)
  waiting for transfers between devices  4.98 us (5%)
  matrix products  2.79 us (3%)
    scatter-add x1, other arithmetic, on_device(): surface = empty_field.at[:, landing].add(received, mode='drop')  23.2 us
    psum x1, blocking collectives, on_device(): panel_source = lax.psum(partial_value, 'obs')  17.3 us
    unnamed x15, local copies, waits for them, and re-layouts  6.53 us
    all_to_all x1, starting transfers between devices, on_device(): lax.all_to_all(out_index, 'cells', split_axis=1, concat_axis=1, tiled=True)  5.2 us
    ppermute x2, starting transfers between devices, extended(): lax.ppermute(tail, axis, [(i, (i + 1) % count) for i in range(ends)])  5.15 us
    all_to_all x1, waiting for transfers between devices, on_device(): lax.all_to_all(outgoing, 'cells', split_axis=1, concat_axis=1, tiled=True)  4.97 us
    scatter x1, local copies, waits for them, and re-layouts, on_device(): jnp.zeros((COMP, devices * capacity), jnp.float32).at[:, slot_of]  3.59 us
    all_to_all x1, starting transfers between devices, on_device(): lax.all_to_all(outgoing, 'cells', split_axis=1, concat_axis=1, tiled=True)  3.38 us
  transfers between devices with their start and end apart: 6, of which 1 were waited for; matrix products, arithmetic and copies ran while one was open for 43% of the time, Pallas kernels for 0%

commit v1 on v0

--- a/solution.py
+++ b/solution.py
@@ -8,6 +8,12 @@
 COMP = 5
 TILE = 128
 smoothing = 0.25
+
+
+def summed_here(x, mesh_axis):
+    parts = lax.all_gather(x, mesh_axis, axis=0, tiled=False)
+    total = parts.sum(axis=0)
+    return total
 
 
 def extended(cells, sides, width, closed):
@@ -52,7 +58,7 @@
     )
     projected = projected.reshape(projected.shape[0], -1)
     partial_value = jnp.sum(amplitude.astype(jnp.float32) * projected[:, None, :], axis=0)
-    panel_source = lax.psum(partial_value, "obs")
+    panel_source = summed_here(partial_value, "obs")
     my_block = lax.axis_index("cells")
     my_group = lax.axis_index("obs")
     azimuth_local = adjoint.shape[1]

time: 94.1 us -> 90.5 us (0.962)
  blocking collectives: 17.3 us -> 13.8 us
    psum x1 -> x0, blocking collectives: 17.3 us -> none  [on_device(): panel_source = lax.psum(partial_value, 'obs')]
    all_gather x0 -> x1, blocking collectives: none -> 13.8 us  [summed_here(): parts = lax.all_gather(x, mesh_axis, axis=0, tiled=False)]
  transfers between devices with their start and end apart: 6 -> 6, of which waited for: 1 -> 1; matrix products, arithmetic and copies ran while one was open for 43% -> 45% of each run, Pallas kernels for 0% -> 0%
where the time goes in v1:
time: 90.5 us; the launch traced here: 89.5 us
  other arithmetic  33.4 us (37%)
  starting transfers between devices  17.1 us (19%)
  local copies, waits for them, and re-layouts  16.5 us (18%)
  blocking collectives  13.8 us (15%)
  waiting for transfers between devices  4.98 us (6%)
  matrix products  2.79 us (3%)
  between operations  0.93 us (1%)
    scatter-add x1, other arithmetic, on_device(): surface = empty_field.at[:, landing].add(received, mode='drop')  23.2 us
    all_gather x1, blocking collectives, summed_here(): parts = lax.all_gather(x, mesh_axis, axis=0, tiled=False)  13.8 us
    unnamed x15, local copies, waits for them, and re-layouts  6.53 us
    all_to_all x1, starting transfers between devices, on_device(): lax.all_to_all(out_index, 'cells', split_axis=1, concat_axis=1, tiled=True)  5.2 us
    ppermute x2, starting transfers between devices, extended(): lax.ppermute(tail, axis, [(i, (i + 1) % count) for i in range(ends)])  5.15 us
    all_to_all x1, waiting for transfers between devices, on_device(): lax.all_to_all(outgoing, 'cells', split_axis=1, concat_axis=1, tiled=True)  4.97 us
    scatter x1, local copies, waits for them, and re-layouts, on_device(): jnp.zeros((COMP, devices * capacity), jnp.float32).at[:, slot_of]  3.59 us
    all_to_all x1, starting transfers between devices, on_device(): lax.all_to_all(outgoing, 'cells', split_axis=1, concat_axis=1, tiled=True)  3.38 us
  transfers between devices with their start and end apart: 6, of which 1 were waited for; matrix products, arithmetic and copies ran while one was open for 45% of the time, Pallas kernels for 0%

profile of v1, /device:TPU:0, one launch (start us, length us, event | category | flops | bytes accessed | tf_op | source)
XLA Modules:
  0.0 89.5 jit_solution(16178902901365809895)
XLA Ops:
  0.6 0.8 fusion.22
  1.4 2.3 %reduce-window.6 = s32[8,8,128]{2,1,0:T(8,128)S(1)} reduce-window(s32[8,8,128]{2,1,0:T(8,128)S(1)} %fusion.22, s32[]{:T(128)} %constant.118.clone.1), window={size=1x1x128 pad=0_0x0_0x127_0}, to_apply=%region_0.1 | reduce-window | flops 1040384 | bytes 65540 | tf_op jit(solution)/shard_map/reduce-window
  4.2 0.7 fusion.21
  5.6 0.7 fusion.25
  6.3 0.7 and_reduce_fusion
  7.1 4.9 %scatter_custom_fusion.2 = s32[4096]{0:T(1024)} fusion(s32[1024]{0:T(1024)S(1)} %broadcast_select_fusion, s32[1024]{0:T(1024)S(1)} %get-tuple-element.25, s32[]{:T(128)} %constant.116.clone.1), kind=kCustom, calls=%fused_computation.79 | custom fusion | bytes 16388
  12.0 5.2 %all-to-all-start = ((s32[1,8,512]{2,0,1:T(1,128)}), s32[1,8,512]{2,0,1:T(1,128)S(1)}, u32[]{:S(2)}, u32[]{:S(2)}) async-start(s32[1,8,512]{2,0,1:T(1,128)} %bitcast.12), calls=%async_computation | async-start | bytes 32768 | tf_op jit(solution)/shard_map/all_to_all | solution.py:83
  17.2 0.9 %copy.91 = f32[5,2,16,128]{3,0,2,1:T(8,128)S(1)} copy(f32[5,2,16,128]{3,2,1,0:T(8,128)} %param.15) | data formatting | bytes 163840 | tf_op args[6]
  18.1 1.3 %collective-permute-start.2 = (f32[5,2,1,128]{3,0,2,1:T(8,128)S(1)}, f32[5,2,1,128]{3,0,2,1:T(8,128)}, u32[]{:S(2)}, u32[]{:S(2)}) collective-permute-start(f32[5,2,1,128]{3,0,2,1:T(8,128)S(1)} %get-tuple-element.13), channel_id=1, source_target_pairs={{1,0},{2,1},{3,2},{5,4},{6,5},{7,6},{9,8},{10,9},{11,10},{13,12},{... | collective-permute-start | bytes 15368 | tf_op jit(solution)/shard_map/ppermute | solution.py:29
  19.4 5.1 %collective-permute-start.3 = (f32[5,2,1,128]{3,0,2,1:T(8,128)S(1)}, f32[5,2,1,128]{3,0,2,1:T(8,128)}, u32[]{:S(2)}, u32[]{:S(2)}) collective-permute-start(f32[5,2,1,128]{3,0,2,1:T(8,128)S(1)} %get-tuple-element.12), channel_id=1, source_target_pairs={{0,1},{1,2},{2,3},{4,5},{5,6},{6,7},{8,9},{9,10},{10,11},{12,13},{... | collective-permute-start | bytes 15368 | tf_op jit(solution)/shard_map/ppermute | solution.py:27
  25.2 2.1 %collective-permute-start = (f32[5,1,16,128]{3,0,2,1:T(8,128)}, f32[5,1,16,128]{3,0,2,1:T(8,128)S(1)}, u32[]{:S(2)}, u32[]{:S(2)}) collective-permute-start(f32[5,1,16,128]{3,0,2,1:T(8,128)} %get-tuple-element.11), channel_id=1, source_target_pairs={{4,0},{8,4},{12,8},{16,12},{20,16},{24,20},{28,24},{0,28},{5,1},{9... | collective-permute-start | bytes 122888 | tf_op jit(solution)/shard_map/ppermute | solution.py:29
  28.0 0.8 slice.95
  28.8 0.8 pad_select_fusion.6
  29.7 0.9 pad_select_fusion.5
  30.7 0.8 pad_select_fusion.4
  32.7 1.1 %fusion.10 = f32[5,2,16,128]{3,0,2,1:T(8,128)} fusion(f32[5,2,16,128]{3,0,2,1:T(8,128)S(1)} %copy.91, f32[1,1,5,5]{3,0,2,1:T(1,128)S(1)} %get-tuple-element.16), kind=kOutput, calls=%fused_computation.16 | convolution fusion | flops 1372160 | bytes 346624 | tf_op jit(solution)/shard_map/kc,karz->carz/dot_general | solution.py:107
  33.8 13.8 %all-gather.1 = f32[4,5,1024]{2,1,0:T(8,128)S(1)} all-gather(f32[1,5,1024]{2,1,0:T(8,128)S(1)} %bitcast.78), channel_id=2, replica_groups=mesh['cells'=8,'obs'=4] {'obs'}, dimensions={0}, use_global_device_ids=true | all-gather | bytes 102400 | tf_op jit(solution)/shard_map/all_gather | solution.py:14
  47.8 3.6 %scatter_custom_fusion = f32[5,4096]{0,1:T(8,128)S(1)} fusion(s32[1024]{0:T(1024)S(1)} %get-tuple-element.26, f32[1024,5]{1,0:T(8,128)S(1)} %copy.93, f32[]{:T(128)} %constant.115.clone.1), kind=kCustom, calls=%fused_computation.20 | custom fusion | bytes 81924 | tf_op jit(solution)/shard_map/scatter | solution.py:79
  51.4 1.3 %copy.94 = f32[5,8,512]{2,0,1:T(8,128)} copy(f32[5,8,512]{0,2,1:T(8,128)S(1)} %bitcast.74) | data formatting | bytes 163840 | tf_op jit(solution)/shard_map/all_to_all | solution.py:82
  52.7 1.1 %fusion.9 = f32[5,2,16,128]{3,0,2,1:T(8,128)S(1)} fusion(f32[5,2,1,128]{3,0,2,1:T(8,128)} %collective-permute-done.2, f32[5,2,16,128]{3,0,2,1:T(8,128)S(1)} %copy.91, f32[5,2,1,128]{3,0,2,1:T(8,128)} %collective-permute-done.3, f32[1,1,5,5]{3,0,2,1:T(1,128)S(1)} %get-tuple-element.15), kind=kOutput, calls=%fused_computation.15 | convolution fusion | flops 1454080 | bytes 174180 | tf_op jit(solution)/shard_map/kc,karz->carz/dot_general | solution.py:107
  53.8 3.4 %all-to-all-start.1 = ((f32[5,8,512]{2,0,1:T(8,128)}), f32[5,8,512]{2,0,1:T(8,128)S(1)}, u32[]{:S(2)}, u32[]{:S(2)}) async-start(f32[5,8,512]{2,0,1:T(8,128)} %copy.94), calls=%async_computation.1 | async-start | bytes 262144 | tf_op jit(solution)/shard_map/all_to_all | solution.py:82
  57.7 5.0 %all-to-all-done.1 = f32[5,8,512]{2,0,1:T(8,128)S(1)} async-done(((f32[5,8,512]{2,0,1:T(8,128)}), f32[5,8,512]{2,0,1:T(8,128)S(1)}, u32[]{:S(2)}, u32[]{:S(2)}) %all-to-all-start.1) | async-done | bytes 81952 | tf_op jit(solution)/shard_map/all_to_all | solution.py:82
  62.7 2.0 %copy.95 = f32[4096,5]{1,0:T(8,128)} copy(f32[4096,5]{0,1:T(8,128)S(1)} %bitcast.75) | data formatting | bytes 163840 | tf_op jit(solution)/shard_map/all_to_all | solution.py:82
  64.6 23.2 %scatter_custom_fusion.1 = f32[5,4096]{0,1:T(8,128)S(1)} fusion(s32[4096]{0:T(1024)S(1)} %bitcast.84, f32[4096,5]{1,0:T(8,128)} %copy.95, f32[]{:T(128)} %constant.115.clone.1), kind=kCustom, calls=%fused_computation.18 | custom fusion | flops 20480 | bytes 82432 | tf_op jit(solution)/shard_map/scatter-add | solution.py:94
  (48 shorter events, 6.3 us)
Async XLA Ops:
  0.6 31.7 %copy-start = (bf16[1024,256]{1,0:T(8,128)(2,1)S(1)}, bf16[1024,256]{1,0:T(8,128)(2,1)}, u32[]{:S(2)}) copy-start(bf16[1024,256]{1,0:T(8,128)(2,1)} %param.11) | copy-start | bytes 1572868
  12.0 41.8 %all-to-all-start = ((s32[1,8,512]{2,0,1:T(1,128)}), s32[1,8,512]{2,0,1:T(1,128)S(1)}, u32[]{:S(2)}, u32[]{:S(2)}) async-start(s32[1,8,512]{2,0,1:T(1,128)} %bitcast.12), calls=%async_computation | async-start | bytes 32768 | tf_op jit(solution)/shard_map/all_to_all | solution.py:83
  18.1 34.6 %collective-permute-start.2 = (f32[5,2,1,128]{3,0,2,1:T(8,128)S(1)}, f32[5,2,1,128]{3,0,2,1:T(8,128)}, u32[]{:S(2)}, u32[]{:S(2)}) collective-permute-start(f32[5,2,1,128]{3,0,2,1:T(8,128)S(1)} %get-tuple-element.13), channel_id=1, source_target_pairs={{1,0},{2,1},{3,2},{5,4},{6,5},{7,6},{9,8},{10,9},{11,10},{13,12},{... | collective-permute-start | bytes 15368 | tf_op jit(solution)/shard_map/ppermute | solution.py:29
  19.4 33.3 %collective-permute-start.3 = (f32[5,2,1,128]{3,0,2,1:T(8,128)S(1)}, f32[5,2,1,128]{3,0,2,1:T(8,128)}, u32[]{:S(2)}, u32[]{:S(2)}) collective-permute-start(f32[5,2,1,128]{3,0,2,1:T(8,128)S(1)} %get-tuple-element.12), channel_id=1, source_target_pairs={{0,1},{1,2},{2,3},{4,5},{5,6},{6,7},{8,9},{9,10},{10,11},{12,13},{... | collective-permute-start | bytes 15368 | tf_op jit(solution)/shard_map/ppermute | solution.py:27
  25.2 63.2 %collective-permute-start = (f32[5,1,16,128]{3,0,2,1:T(8,128)}, f32[5,1,16,128]{3,0,2,1:T(8,128)S(1)}, u32[]{:S(2)}, u32[]{:S(2)}) collective-permute-start(f32[5,1,16,128]{3,0,2,1:T(8,128)} %get-tuple-element.11), channel_id=1, source_target_pairs={{4,0},{8,4},{12,8},{16,12},{20,16},{24,20},{28,24},{0,28},{5,1},{9... | collective-permute-start | bytes 122888 | tf_op jit(solution)/shard_map/ppermute | solution.py:29
  27.3 61.1 %collective-permute-start.1 = (f32[5,1,16,128]{3,0,2,1:T(8,128)S(1)}, f32[5,1,16,128]{3,0,2,1:T(8,128)S(1)}, u32[]{:S(2)}, u32[]{:S(2)}) collective-permute-start(f32[5,1,16,128]{3,0,2,1:T(8,128)S(1)} %get-tuple-element.10), channel_id=1, source_target_pairs={{0,4},{4,8},{8,12},{12,16},{16,20},{20,24},{24,28},{28,0},{1,5},{5... | collective-permute-start | bytes 122888 | tf_op jit(solution)/shard_map/ppermute | solution.py:27
  28.8 3.9 %copy-start.5 = (f32[1,3,5,5]{3,0,2,1:T(1,128)S(1)}, f32[1,3,5,5]{3,0,2,1:T(1,128)}, u32[]{:S(2)}) copy-start(f32[1,3,5,5]{3,0,2,1:T(1,128)} %param.17) | copy-start | bytes 904
  29.7 4.0 %copy-start.1 = (bf16[16,5,1024]{2,0,1:T(8,128)(2,1)S(1)}, bf16[16,5,1024]{2,0,1:T(8,128)(2,1)}, u32[]{:S(2)}) copy-start(bf16[16,5,1024]{2,0,1:T(8,128)(2,1)} %param.10) | copy-start | bytes 491524
  47.6 5.1 %copy-start.2 = (f32[5,1024]{1,0:T(8,128)}, f32[5,1024]{1,0:T(8,128)S(1)}, u32[]{:S(2)}) copy-start(f32[5,1024]{1,0:T(8,128)S(1)} %reduce_sum.29) | copy-start | bytes 61444
  53.8 8.8 %all-to-all-start.1 = ((f32[5,8,512]{2,0,1:T(8,128)}), f32[5,8,512]{2,0,1:T(8,128)S(1)}, u32[]{:S(2)}, u32[]{:S(2)}) async-start(f32[5,8,512]{2,0,1:T(8,128)} %copy.94), calls=%async_computation.1 | async-start | bytes 262144 | tf_op jit(solution)/shard_map/all_to_all | solution.py:82
  64.6 23.8 %copy-start.3 = (f32[5,2,16,128]{3,0,2,1:T(8,128)S(1)}, f32[5,2,16,128]{3,0,2,1:T(8,128)}, u32[]{:S(2)}) copy-start(f32[5,2,16,128]{3,0,2,1:T(8,128)} %fusion.10) | copy-start | bytes 245764
  64.6 23.8 %copy-start.4 = (f32[2,16,128]{2,1,0:T(8,128)S(1)}, f32[2,16,128]{2,1,0:T(8,128)}, u32[]{:S(2)}) copy-start(f32[2,16,128]{2,1,0:T(8,128)} %param.16) | copy-start | bytes 49156
